TPU v7x, 32 devices: a whole 2x2x4 slice. The times are simulated.
32 devices in a mesh: dp: 4 (over y, x), seq: 8 (over z, core).
Axes of the slice: x: 2, y: 2, z: 4, core: 2. Of those that a mesh axis runs over, the one named last changes fastest.
Arguments:
- tiles: bfloat16 [4, 8192, 768], P('dp', 'seq'), may hold values from -48 to 48
- tile_count: int32 [4], P('dp'), may hold values from 4097 to 8192
- offsets: int32 [16], replicated, may hold values from 0 to 15
- w_query: bfloat16 [768, 768], replicated, may hold values from -0.375 to 0.375
- w_key: bfloat16 [768, 768], replicated, may hold values from -0.375 to 0.375
- w_value: bfloat16 [768, 768], replicated, may hold values from -0.21875 to 0.21875
- w_out: bfloat16 [768, 768], replicated, may hold values from -0.21875 to 0.21875
- cotangent: bfloat16 [4, 8192, 768], P('dp', 'seq'), may hold values from -0.046875 to 0.046875
Outputs:
- branch: bfloat16 [4, 8192, 768], P('dp', 'seq')
- grad_out: float32 [768, 768], P(None, 'seq')
All inputs are finite; a program needn't handle non-finite values.
Results may differ from a plain program's by a relative error of at most 0.0095.
The roundings to bfloat16 on the way count: a program that leaves them out, or rounds other values in their place, can miss the bound.
Values may be sent and summed in bfloat16 or wider, within the bound.
A program may use at most 128 MiB of HBM per device.

v0:
```python
import jax
import jax.numpy as jnp
from jax import lax
from jax.sharding import PartitionSpec as P

D = 768
ATTENTION_HEADS = 16
HEAD_SIZE = 48
SEG = 1024
RATE = 16
NEGATIVE_FLOOR = -1e30
head_group = 4


def project(inputs, weight):
    return jnp.dot(inputs, weight, preferred_element_type=jnp.float32).astype(jnp.bfloat16)


def select_rows(tensor, offsets):
    segment_height = tensor.shape[0]
    grouped = tensor.reshape(segment_height // RATE, RATE, ATTENTION_HEADS, HEAD_SIZE)
    onehot = (jnp.arange(RATE, dtype=jnp.int32)[:, None] == offsets[None, :]).astype(jnp.bfloat16)
    return jnp.einsum("arhd,rh->ahd", grouped, onehot, preferred_element_type=jnp.float32).astype(
        jnp.bfloat16
    )


def local_attention(query_proj, key_proj, value_proj, is_live):
    segment_height = query_proj.shape[0]
    segments = segment_height // SEG
    groups = ATTENTION_HEADS // head_group
    query_seg = query_proj.reshape(segments, SEG, groups, head_group, HEAD_SIZE)
    key_seg = key_proj.reshape(segments, SEG, groups, head_group, HEAD_SIZE)
    value_seg = value_proj.reshape(segments, SEG, groups, head_group, HEAD_SIZE)
    alive_seg = is_live.reshape(segments, SEG)

    def one_group(index):
        query_part = lax.dynamic_index_in_dim(query_seg, index, 2, keepdims=False)
        key_part = lax.dynamic_index_in_dim(key_seg, index, 2, keepdims=False)
        value_part = lax.dynamic_index_in_dim(value_seg, index, 2, keepdims=False)
        scores = jnp.einsum(
            "sqhd,skhd->shqk", query_part, key_part, preferred_element_type=jnp.float32
        ) * HEAD_SIZE ** (-0.5)
        scores = jnp.where(alive_seg[:, None, None, :], scores, NEGATIVE_FLOOR)
        maxima = jnp.max(scores, axis=-1)
        weights = jnp.exp(scores - maxima[..., None])
        totals = jnp.sum(weights, axis=-1)
        weighted = jnp.einsum(
            "shqk,skhd->sqhd",
            weights.astype(jnp.bfloat16),
            value_part,
            preferred_element_type=jnp.float32,
        )
        return (maxima, totals, weighted)

    maxima, totals, weighted = lax.map(one_group, jnp.arange(groups, dtype=jnp.int32))
    maxima = maxima.transpose(1, 3, 0, 2).reshape(segment_height, ATTENTION_HEADS)
    totals = totals.transpose(1, 3, 0, 2).reshape(segment_height, ATTENTION_HEADS)
    weighted = weighted.transpose(1, 2, 0, 3, 4).reshape(segment_height, ATTENTION_HEADS, HEAD_SIZE)
    return (maxima, totals, weighted)


def combine(local, dilated_branch, offsets, is_live):
    local_max, local_total, local_sum = local
    dilated_row_max, dilated_value_total, dilated_row_sum = dilated_branch
    segment_height = local_max.shape[0]
    dilation_match = jnp.arange(RATE, dtype=jnp.int32)[:, None] == offsets[None, :]
    dense_row_max = jnp.where(
        dilation_match[None], dilated_row_max[:, None, :], NEGATIVE_FLOOR
    ).reshape(segment_height, ATTENTION_HEADS)
    dense_value_total = jnp.where(
        dilation_match[None], dilated_value_total[:, None, :], 0.0
    ).reshape(segment_height, ATTENTION_HEADS)
    dense_row_sum = jnp.where(
        dilation_match[None, :, :, None], dilated_row_sum[:, None], 0.0
    ).reshape(segment_height, ATTENTION_HEADS, HEAD_SIZE)
    top = jnp.maximum(local_max, dense_row_max)
    near = jnp.exp(local_max - top)
    far = jnp.exp(dense_row_max - top)
    attn = (near[..., None] * local_sum + far[..., None] * dense_row_sum) / (
        near * local_total + far * dense_value_total
    )[..., None]
    attn = jnp.where(is_live[:, None, None], attn, 0.0)
    return attn.reshape(segment_height, D).astype(jnp.bfloat16)


def body(tiles, tile_count, offsets, w_query, w_key, w_value, w_out, cotangent):
    inputs = tiles[0]
    segment_height = inputs.shape[0]
    shard_rank = lax.axis_index("seq")
    live_count = tile_count[0]
    query_proj = project(inputs, w_query).reshape(segment_height, ATTENTION_HEADS, HEAD_SIZE)
    key_proj = project(inputs, w_key).reshape(segment_height, ATTENTION_HEADS, HEAD_SIZE)
    value_proj = project(inputs, w_value).reshape(segment_height, ATTENTION_HEADS, HEAD_SIZE)
    positions = shard_rank * segment_height + jnp.arange(segment_height, dtype=jnp.int32)
    is_live = positions < live_count
    local = local_attention(query_proj, key_proj, value_proj, is_live)
    picked = segment_height // RATE
    query_sel = select_rows(query_proj, offsets)
    key_sel = select_rows(key_proj, offsets)
    value_sel = select_rows(value_proj, offsets)
    score_scale = HEAD_SIZE ** (-0.5)
    portion = (
        lax.all_gather(key_sel.reshape(picked, D), "seq", axis=0, tiled=True),
        lax.all_gather(value_sel.reshape(picked, D), "seq", axis=0, tiled=True),
    )
    old_max = jnp.full((picked, ATTENTION_HEADS), NEGATIVE_FLOOR, jnp.float32)
    key_part = portion[0].reshape(portion[0].shape[0], ATTENTION_HEADS, HEAD_SIZE)
    value_part = portion[1].reshape(portion[1].shape[0], ATTENTION_HEADS, HEAD_SIZE)
    amount = key_part.shape[0]
    key_live = jnp.arange(amount, dtype=jnp.int32)[:, None] * RATE + offsets[None, :] < live_count
    scores = (
        jnp.einsum("qhd,khd->qhk", query_sel, key_part, preferred_element_type=jnp.float32)
        * score_scale
    )
    scores = jnp.where(key_live.T[None], scores, NEGATIVE_FLOOR)
    new_max = jnp.maximum(old_max, jnp.max(scores, axis=-1))
    weights = jnp.exp(scores - new_max[..., None])
    new_total = jnp.sum(weights, axis=-1)
    new_sum = jnp.einsum(
        "qhk,khd->qhd", weights.astype(jnp.bfloat16), value_part, preferred_element_type=jnp.float32
    )
    dilated_branch = (new_max, new_total, new_sum)
    attn = combine(local, dilated_branch, offsets, is_live)
    branch = jnp.dot(attn, w_out, preferred_element_type=jnp.float32).astype(jnp.bfloat16)[None]
    gradient_in = cotangent[0]
    shares = lax.psum_scatter(
        jnp.einsum("tc,td->cd", gradient_in, attn, preferred_element_type=jnp.float32),
        "seq",
        scatter_dimension=0,
        tiled=True,
    )
    grad_part = lax.psum(shares.astype(jnp.bfloat16), "dp").astype(jnp.float32).T
    return (branch, grad_part)


def solution(mesh):
    in_specs = (P("dp", "seq", None), P("dp"), P(), P(), P(), P(), P(), P("dp", "seq", None))
    out_specs = (P("dp", "seq", None), P(None, "seq"))
    return jax.shard_map(body, mesh=mesh, in_specs=in_specs, out_specs=out_specs, check_vma=False)
```

profile of v0, /device:TPU:0, one launch (start us, length us, event | category | flops | bytes accessed | tf_op | source)
XLA Modules:
  0.0 290.6 jit_solution(8163011718679875207)
XLA Ops:
  7.2 0.6 iota_multiply_fusion
  8.5 0.7 iota_compare_fusion
  9.7 2.8 convolution_convert_fusion.3
  12.5 2.6 convolution_convert_fusion.2
  15.1 2.6 convolution_convert_fusion.1
  17.7 2.8 copy.49
  20.4 1.6 copy.45
  22.1 1.6 copy.47
  23.6 7.2 %reshape_reshape.22 = bf16[64,16,16,48]{3,2,1,0:T(8,128)(2,1)} reshape(bf16[1024,768]{1,0:T(8,128)(2,1)} %copy.47) | data formatting | bytes 3145728 | tf_op jit(solution)/shard_map/reshape;reshape | solution.py:21
  30.8 7.2 %reshape_reshape.21 = bf16[64,16,16,48]{3,2,1,0:T(8,128)(2,1)} reshape(bf16[1024,768]{1,0:T(8,128)(2,1)} %copy.45) | data formatting | bytes 3145728 | tf_op jit(solution)/shard_map/reshape;reshape | solution.py:21
  38.0 7.2 %reshape_reshape.23 = bf16[64,16,16,48]{3,2,1,0:T(8,128)(2,1)} reshape(bf16[1024,768]{1,0:T(8,128)(2,1)} %copy.49) | data formatting | bytes 3145728 | tf_op jit(solution)/shard_map/reshape;reshape | solution.py:21
  45.2 9.0 %multiply_reduce_fusion.1 = (bf16[16,64,48]{2,0,1:T(8,128)(2,1)S(1)}, bf16[16,64,48]{2,0,1:T(8,128)(2,1)}, bf16[16,64,48]{2,0,1:T(8,128)(2,1)}) fusion(f32[16,16]{0,1:T(8,128)S(1)} %copy.80, bf16[64,16,16,48]{3,2,1,0:T(8,128)(2,1)} %reshape_reshape.22, bf16[64,16,16,48]{3,2,1,0:T(8,128)(2,1)} %reshape_reshape.23, bf16[64,16,16,48]{3,2,1,0:T(8,128)(2,1)} %reshape_reshape.21), kind=kLoop, calls=%fused_computation.25 | loop fusion | flops 6930432 | bytes 5014528
  54.1 0.9 copy.70
  55.1 1.2 reshape.266
  56.3 1.2 reshape.263
  57.5 18.4 %all_gather.6 = bf16[512,768]{1,0:T(8,128)(2,1)} all-gather(bf16[64,768]{1,0:T(8,128)(2,1)S(1)} %reshape.263), channel_id=1, replica_groups=mesh['dp'=4,'seq'=8] {'seq'}, dimensions={0}, use_global_device_ids=true | all-gather | bytes 884736 | tf_op jit(solution)/shard_map/all_gather | solution.py:104
  76.0 2.3 copy.46
  78.3 16.6 %all_gather.7 = bf16[512,768]{1,0:T(8,128)(2,1)} all-gather(bf16[64,768]{1,0:T(8,128)(2,1)S(1)} %reshape.266), channel_id=1, replica_groups=mesh['dp'=4,'seq'=8] {'seq'}, dimensions={0}, use_global_device_ids=true | all-gather | bytes 884736 | tf_op jit(solution)/shard_map/all_gather | solution.py:105
  94.9 2.3 copy.50
  97.3 1.8 bitcast_reduce_fusion
  99.1 1.4 fusion.34
  100.5 0.6 convolution_bitcast_fusion.1
  101.1 1.0 copy.51
  102.1 1.7 broadcast_in_dim.151
  103.8 1.3 broadcast_in_dim.152
  105.1 1.7 broadcast_in_dim.159
  106.8 1.3 broadcast_in_dim.160
  108.7 66.5 %while.15 = (s32[]{:T(128)}, f32[4,1,4,1024]{3,2,1,0:T(4,128)}, f32[4,1,4,1024]{3,2,1,0:T(4,128)}, f32[4,1,1024,4,48]{2,4,3,1,0:T(8,128)}, s32[4]{0:T(128)S(1)},...) while((s32[]{:T(128)}, f32[4,1,4,1024]{3,2,1,0:T(4,128)}, ...), condition=%wide.region_3.4_spmd.clone, body=%wide.region_0.3_spmd.clone.sunk | while | flops 851437568 | bytes 52434116 | solution.py:56
  108.7 0.6 dynamic_slice.41
  111.0 0.7 add_compare_fusion.4
  111.6 3.3 %fusion.70 = (f32[4,1024]{1,0:T(4,128)S(1)}, f32[4,1024,1024]{1,2,0:T(8,128)S(1)}) fusion(pred[1024]{0:T(1024)(128)(4,1)S(1)} %add_compare_fusion.4, bf16[1,1024,4,4,48]{1,4,3,2,0:T(8,128)(2,1)S(1)} %get-tuple-element.223, s32[]{:T(128)S(6)} %select_n.128, bf16[1,1024,4,4,48]{1,4,3,2,0:T(8,128)(2,1)S(1)} %get-tuple-element.222), kind=kOutput, calls=%fused_computation.3.clone.1 | convolution fusion | flops 415232000 | bytes 17582080 | tf_op jit(solution)/shard_map/while/body/eval_jaxpr/sqhd,skhd->shqk/dot_general | solution.py:41
  115.0 4.1 %fusion.71 = f32[4,1024]{1,0:T(4,128)S(1)} fusion(f32[4,1024,1024]{1,2,0:T(8,128)S(1)} %get-tuple-element.187, f32[4,1024]{1,0:T(4,128)S(1)} %get-tuple-element.188, pred[1024]{0:T(1024)(128)(4,1)S(1)} %add_compare_fusion.4), kind=kLoop, calls=%fused_computation.5.clone.1 | loop fusion | flops 16773120 | bytes 16811008 | tf_op jit(solution)/shard_map/while/body/eval_jaxpr/reduce_sum | solution.py:47
  119.1 5.7 %fusion.72 = f32[4,1,1024,4,48]{2,4,3,1,0:T(8,128)} fusion(f32[4,1,1024,4,48]{2,4,3,1,0:T(8,128)} %get-tuple-element.207, s32[]{:T(128)S(6)} %copy.89, f32[4,1024,1024]{1,2,0:T(8,128)S(1)} %get-tuple-element.187, f32[4,1024]{1,0:T(4,128)S(1)} %get-tuple-element.188, pred[1024]{0:T(1024)(128)(4,1)S(1)} %add_compare_fusion.4, ...), kind=kOutput, calls=%fused_computation.9.clone.1 | convolution fusion | flops 419430400 | bytes 17974280 | tf_op jit(solution)/shard_map/while/body/eval_jaxpr/shqk,skhd->sqhd/dot_general | solution.py:48
  124.8 0.6 bitcast_dynamic-update-slice_fusion.3
  127.6 0.7 add_compare_fusion.4
  128.3 3.3 %fusion.70 = (f32[4,1024]{1,0:T(4,128)S(1)}, f32[4,1024,1024]{1,2,0:T(8,128)S(1)}) fusion(pred[1024]{0:T(1024)(128)(4,1)S(1)} %add_compare_fusion.4, bf16[1,1024,4,4,48]{1,4,3,2,0:T(8,128)(2,1)S(1)} %get-tuple-element.223, s32[]{:T(128)S(6)} %select_n.128, bf16[1,1024,4,4,48]{1,4,3,2,0:T(8,128)(2,1)S(1)} %get-tuple-element.222), kind=kOutput, calls=%fused_computation.3.clone.1 | convolution fusion | flops 415232000 | bytes 17582080 | tf_op jit(solution)/shard_map/while/body/eval_jaxpr/sqhd,skhd->shqk/dot_general | solution.py:41
  131.6 4.1 %fusion.71 = f32[4,1024]{1,0:T(4,128)S(1)} fusion(f32[4,1024,1024]{1,2,0:T(8,128)S(1)} %get-tuple-element.187, f32[4,1024]{1,0:T(4,128)S(1)} %get-tuple-element.188, pred[1024]{0:T(1024)(128)(4,1)S(1)} %add_compare_fusion.4), kind=kLoop, calls=%fused_computation.5.clone.1 | loop fusion | flops 16773120 | bytes 16811008 | tf_op jit(solution)/shard_map/while/body/eval_jaxpr/reduce_sum | solution.py:47
  135.8 5.6 %fusion.72 = f32[4,1,1024,4,48]{2,4,3,1,0:T(8,128)} fusion(f32[4,1,1024,4,48]{2,4,3,1,0:T(8,128)} %get-tuple-element.207, s32[]{:T(128)S(6)} %copy.89, f32[4,1024,1024]{1,2,0:T(8,128)S(1)} %get-tuple-element.187, f32[4,1024]{1,0:T(4,128)S(1)} %get-tuple-element.188, pred[1024]{0:T(1024)(128)(4,1)S(1)} %add_compare_fusion.4, ...), kind=kOutput, calls=%fused_computation.9.clone.1 | convolution fusion | flops 419430400 | bytes 17974280 | tf_op jit(solution)/shard_map/while/body/eval_jaxpr/shqk,skhd->sqhd/dot_general | solution.py:48
  141.4 0.6 bitcast_dynamic-update-slice_fusion.3
  144.2 0.7 add_compare_fusion.4
  144.9 3.3 %fusion.70 = (f32[4,1024]{1,0:T(4,128)S(1)}, f32[4,1024,1024]{1,2,0:T(8,128)S(1)}) fusion(pred[1024]{0:T(1024)(128)(4,1)S(1)} %add_compare_fusion.4, bf16[1,1024,4,4,48]{1,4,3,2,0:T(8,128)(2,1)S(1)} %get-tuple-element.223, s32[]{:T(128)S(6)} %select_n.128, bf16[1,1024,4,4,48]{1,4,3,2,0:T(8,128)(2,1)S(1)} %get-tuple-element.222), kind=kOutput, calls=%fused_computation.3.clone.1 | convolution fusion | flops 415232000 | bytes 17582080 | tf_op jit(solution)/shard_map/while/body/eval_jaxpr/sqhd,skhd->shqk/dot_general | solution.py:41
  148.3 4.1 %fusion.71 = f32[4,1024]{1,0:T(4,128)S(1)} fusion(f32[4,1024,1024]{1,2,0:T(8,128)S(1)} %get-tuple-element.187, f32[4,1024]{1,0:T(4,128)S(1)} %get-tuple-element.188, pred[1024]{0:T(1024)(128)(4,1)S(1)} %add_compare_fusion.4), kind=kLoop, calls=%fused_computation.5.clone.1 | loop fusion | flops 16773120 | bytes 16811008 | tf_op jit(solution)/shard_map/while/body/eval_jaxpr/reduce_sum | solution.py:47
  152.4 5.6 %fusion.72 = f32[4,1,1024,4,48]{2,4,3,1,0:T(8,128)} fusion(f32[4,1,1024,4,48]{2,4,3,1,0:T(8,128)} %get-tuple-element.207, s32[]{:T(128)S(6)} %copy.89, f32[4,1024,1024]{1,2,0:T(8,128)S(1)} %get-tuple-element.187, f32[4,1024]{1,0:T(4,128)S(1)} %get-tuple-element.188, pred[1024]{0:T(1024)(128)(4,1)S(1)} %add_compare_fusion.4, ...), kind=kOutput, calls=%fused_computation.9.clone.1 | convolution fusion | flops 419430400 | bytes 17974280 | tf_op jit(solution)/shard_map/while/body/eval_jaxpr/shqk,skhd->sqhd/dot_general | solution.py:48
  158.0 0.6 bitcast_dynamic-update-slice_fusion.3
  160.9 0.7 add_compare_fusion.4
  161.5 3.3 %fusion.70 = (f32[4,1024]{1,0:T(4,128)S(1)}, f32[4,1024,1024]{1,2,0:T(8,128)S(1)}) fusion(pred[1024]{0:T(1024)(128)(4,1)S(1)} %add_compare_fusion.4, bf16[1,1024,4,4,48]{1,4,3,2,0:T(8,128)(2,1)S(1)} %get-tuple-element.223, s32[]{:T(128)S(6)} %select_n.128, bf16[1,1024,4,4,48]{1,4,3,2,0:T(8,128)(2,1)S(1)} %get-tuple-element.222), kind=kOutput, calls=%fused_computation.3.clone.1 | convolution fusion | flops 415232000 | bytes 17582080 | tf_op jit(solution)/shard_map/while/body/eval_jaxpr/sqhd,skhd->shqk/dot_general | solution.py:41
  164.9 4.1 %fusion.71 = f32[4,1024]{1,0:T(4,128)S(1)} fusion(f32[4,1024,1024]{1,2,0:T(8,128)S(1)} %get-tuple-element.187, f32[4,1024]{1,0:T(4,128)S(1)} %get-tuple-element.188, pred[1024]{0:T(1024)(128)(4,1)S(1)} %add_compare_fusion.4), kind=kLoop, calls=%fused_computation.5.clone.1 | loop fusion | flops 16773120 | bytes 16811008 | tf_op jit(solution)/shard_map/while/body/eval_jaxpr/reduce_sum | solution.py:47
  169.0 5.6 %fusion.72 = f32[4,1,1024,4,48]{2,4,3,1,0:T(8,128)} fusion(f32[4,1,1024,4,48]{2,4,3,1,0:T(8,128)} %get-tuple-element.207, s32[]{:T(128)S(6)} %copy.89, f32[4,1024,1024]{1,2,0:T(8,128)S(1)} %get-tuple-element.187, f32[4,1024]{1,0:T(4,128)S(1)} %get-tuple-element.188, pred[1024]{0:T(1024)(128)(4,1)S(1)} %add_compare_fusion.4, ...), kind=kOutput, calls=%fused_computation.9.clone.1 | convolution fusion | flops 419430400 | bytes 17974280 | tf_op jit(solution)/shard_map/while/body/eval_jaxpr/shqk,skhd->sqhd/dot_general | solution.py:48
  174.6 0.6 bitcast_dynamic-update-slice_fusion.3
  175.2 0.9 reshape.262
  176.1 0.9 reshape.268
  176.9 4.9 %broadcast_in_dim.156 = f32[64,16,16,48]{3,2,1,0:T(8,128)} broadcast(f32[64,16,48]{2,1,0:T(8,128)} %copy.51), dimensions={0,2,3} | broadcast | bytes 3342336 | tf_op jit(solution)/shard_map/jit(_where)/broadcast_in_dim | solution.py:74
  181.9 6.6 %copy.53 = f32[1024,16,48]{0,2,1:T(8,128)} copy(f32[1024,16,48]{2,1,0:T(8,128)} %bitcast.162) | data formatting | bytes 6291456 | tf_op jit(solution)/shard_map/jit(_where)/broadcast_in_dim | solution.py:74
  188.5 4.0 %fusion.32 = bf16[1024,16,48]{0,2,1:T(8,128)(2,1)S(1)} fusion(f32[1024,16,48]{0,2,1:T(8,128)} %copy.53, f32[4,1,1024,4,48]{2,4,3,1,0:T(8,128)} %get-tuple-element.52, f32[1024,16]{0,1:T(8,128)S(1)} %get-tuple-element.111, f32[1024,16]{0,1:T(8,128)S(1)} %get-tuple-element.113, f32[1024,16]{0,1:T(8,128)S(1)} %get-tuple-element.112, ...), kind=kLoop, calls=%fused_computation.37 | loop fusion | flops 5505024 | bytes 8078336 | tf_op jit(solution)/shard_map/convert_element_type | solution.py:84
  192.5 2.9 convolution_bitcast_fusion
  195.4 3.0 %copy.78 = f32[768,768]{1,0:T(8,128)} copy(f32[768,768]{0,1:T(8,128)} %convolution_bitcast_fusion) | data formatting | bytes 4718592
  198.5 7.9 %broadcast_in_dim.157 = f32[1024,768]{1,0:T(8,128)} reshape(f32[64,16,16,48]{3,2,1,0:T(8,128)} %broadcast_in_dim.156) | data formatting | bytes 6291456 | tf_op jit(solution)/shard_map/jit(_where)/broadcast_in_dim | solution.py:74
  206.5 3.6 %copy.52 = f32[1024,768]{0,1:T(8,128)} copy(f32[1024,768]{1,0:T(8,128)} %broadcast_in_dim.157) | data formatting | bytes 6291456 | tf_op jit(solution)/shard_map/jit(_where)/broadcast_in_dim | solution.py:74
  210.0 3.9 %fusion.31 = bf16[1024,768]{0,1:T(8,128)(2,1)S(1)} fusion(f32[1024,768]{0,1:T(8,128)} %copy.52, f32[4,1,1024,4,48]{2,4,3,1,0:T(8,128)} %get-tuple-element.52, f32[1024,16]{0,1:T(8,128)S(1)} %get-tuple-element.111, f32[1024,16]{0,1:T(8,128)S(1)} %get-tuple-element.113, f32[1024,16]{0,1:T(8,128)S(1)} %get-tuple-element.112, ...), kind=kLoop, calls=%fused_computation.36 | loop fusion | flops 5505024 | bytes 8078336 | tf_op jit(solution)/shard_map/convert_element_type | solution.py:84
  213.9 23.1 %reduce-scatter.4.cloned.1.call-done = f32[96,768]{1,0:T(8,128)} async-done(((f32[768,768]{1,0:T(8,128)}), f32[96,768]{1,0:T(8,128)}) %reduce-scatter.4.cloned.1.call-update) | async-done | bytes 294928
  236.9 1.8 copy.79
  238.8 4.0 %fusion.40 = bf16[1,1024,768]{2,1,0:T(8,128)(2,1)} fusion(bf16[1024,768]{0,1:T(8,128)(2,1)S(1)} %fusion.31, bf16[768,768]{1,0:T(8,128)(2,1)} %param.16), kind=kOutput, calls=%fused_computation.53 | convolution fusion | flops 1208745984 | bytes 4325376 | tf_op jit(solution)/shard_map/dot_general | solution.py:125
  242.7 39.3 %all-reduce.2.cloned.1.call-done = bf16[768,96]{1,0:T(8,128)(2,1)} async-done(((bf16[768,96]{1,0:T(8,128)(2,1)}), bf16[768,96]{1,0:T(8,128)(2,1)}) %all-reduce.2.cloned.1.call-update) | async-done | bytes 147472 | tf_op jit(solution)/shard_map/psum | solution.py:133
  282.0 1.8 copy.54
  (44 shorter events, 3.0 us)
Async XLA Ops:
  7.2 2.5 copy-start
  7.2 229.8 %reduce-scatter.4.cloned.1.call-start = ((), (), s32[]{:S(2)}) async-start(), calls=%async_computation.2 | async-start | bytes 2654208
  9.6 2.8 copy-start.11
  12.5 2.6 copy-start.12
  17.7 2.8 copy-start.2
  57.5 39.7 %copy-start.3 = (bf16[16,64,48]{1,2,0:T(8,128)(2,1)S(1)}, bf16[16,64,48]{1,2,0:T(8,128)(2,1)}, u32[]{:S(2)}) copy-start(bf16[16,64,48]{1,2,0:T(8,128)(2,1)} %copy.70) | copy-start | bytes 294916
  76.0 21.2 %copy-start.8 = (s32[512]{0:T(512)S(1)}, s32[512]{0:T(512)}, u32[]{:S(2)}) copy-start(s32[512]{0:T(512)} %iota_multiply_fusion) | copy-start | bytes 6148
  76.0 21.2 %copy-start.9 = (s32[16]{0:T(128)S(1)}, s32[16]{0:T(128)}, u32[]{:S(2)}) copy-start(s32[16]{0:T(128)} %param.12) | copy-start | bytes 196
  97.2 3.2 %copy-start.4 = (bf16[512,768]{0,1:T(8,128)(2,1)S(1)}, bf16[512,768]{0,1:T(8,128)(2,1)}, u32[]{:S(2)}) copy-start(bf16[512,768]{0,1:T(8,128)(2,1)} %copy.50) | copy-start | bytes 2359300
  99.1 1.4 copy-start.5
  181.9 6.6 %copy-start.6 = (pred[1024]{0:T(1024)(128)(4,1)S(1)}, pred[1024]{0:T(1024)(128)(4,1)}, u32[]{:S(2)}) copy-start(pred[1024]{0:T(1024)(128)(4,1)} %add_compare_fusion.2) | copy-start | bytes 3076
  188.5 4.0 %copy-start.10 = (bf16[1,1024,768]{2,1,0:T(8,128)(2,1)S(1)}, bf16[1,1024,768]{2,1,0:T(8,128)(2,1)}, u32[]{:S(2)}) copy-start(bf16[1,1024,768]{2,1,0:T(8,128)(2,1)} %param.17) | copy-start | bytes 4718596
  198.5 83.5 %all-reduce.2.cloned.1.call-start = ((), (), s32[]{:S(2)}) async-start(), calls=%async_computation.1 | async-start | bytes 393216 | tf_op jit(solution)/shard_map/psum | solution.py:133
  206.5 3.6 %copy-start.7 = (pred[1024]{0:T(1024)(128)(4,1)S(1)}, pred[1024]{0:T(1024)(128)(4,1)}, u32[]{:S(2)}) copy-start(pred[1024]{0:T(1024)(128)(4,1)} %add_compare_fusion.2) | copy-start | bytes 3076
  238.7 45.0 %copy-start.1 = (bf16[1,1024,768]{2,1,0:T(8,128)(2,1)S(1)}, bf16[1,1024,768]{2,1,0:T(8,128)(2,1)}, u32[]{:S(2)}) copy-start(bf16[1,1024,768]{2,1,0:T(8,128)(2,1)} %param.10) | copy-start | bytes 4718596
Sparse Core Ops, SparseCore 0:
  198.6 38.3 reduce-scatter.3
  240.4 41.5 all-reduce.1
where the time goes:
time: 292 us; the launch traced here: 291 us
  local copies, waits for them, and re-layouts  79 us (27%)
  waiting for transfers between devices  62.4 us (21%)
  matrix products  53.2 us (18%)
  other arithmetic  39.2 us (13%)
  blocking collectives  35 us (12%)
  between operations  14.9 us (5%)
  loops' own time  6.89 us (2%)
    psum x1, waiting for transfers between devices, body(): lax.psum(shares.astype(jnp.bfloat16), 'dp').astype(jnp.float32)  39.3 us
    unnamed x3, waiting for transfers between devices  23.1 us
    broadcast_in_dim x4, local copies, waits for them, and re-layouts, combine(): jnp.where(dilation_match[None, :, :, None], dilated_row_sum[:, None], 0.0)  23 us
    dot_general x4, matrix products, one_group(): jnp.einsum('shqk,skhd->sqhd', weights.astype(jnp.bfloat16), value_part, p...  22.5 us
    another operation x3, local copies, waits for them, and re-layouts, select_rows(): tensor.reshape(segment_height // RATE, RATE, ATTENTION_HEADS, HEAD_SIZE)  21.5 us
    all_gather x1, blocking collectives, body(): lax.all_gather(key_sel.reshape(picked, D), 'seq', axis=0, tiled=True)  18.4 us
    all_gather x1, blocking collectives, body(): lax.all_gather(value_sel.reshape(picked, D), 'seq', axis=0, tiled=True)  16.6 us
    reduce_sum x4, other arithmetic, one_group(): totals = jnp.sum(weights, axis=-1)  16.4 us
  transfers between devices with their start and end apart: 2, of which 2 were waited for; matrix products, arithmetic and copies ran while one was open for 7% of the time, Pallas kernels for 0%

commit v1 on v0

--- a/solution.py
+++ b/solution.py
@@ -101,7 +101,12 @@
     value_sel = select_rows(value_proj, offsets)
     score_scale = HEAD_SIZE ** (-0.5)
     portion = (
-        lax.all_gather(key_sel.reshape(picked, D), "seq", axis=0, tiled=True),
+        jnp.concatenate(
+            lax.all_to_all(
+                jnp.stack([key_sel.reshape(picked, D)] * lax.axis_size("seq")), "seq", 0, 0
+            ),
+            axis=0,
+        ),
         lax.all_gather(value_sel.reshape(picked, D), "seq", axis=0, tiled=True),
     )
     old_max = jnp.full((picked, ATTENTION_HEADS), NEGATIVE_FLOOR, jnp.float32)

time: 292 us -> 268 us (0.918)
  blocking collectives: 35 us -> 16.1 us
  local copies, waits for them, and re-layouts: 79 us -> 69.1 us
  starting transfers between devices: 0.08 us -> 6.69 us
    all_gather x1 -> x0, blocking collectives: 18.4 us -> none  [body(): lax.all_gather(key_sel.reshape(picked, D), 'seq', axis=0, tiled=True)]
    all_to_all x0 -> x1, starting transfers between devices: none -> 6.35 us  [body(): lax.all_to_all(jnp.stack([key_sel.reshape(picked, D)] * lax.axis_size('se...]
    another operation x0 -> x3, local copies, waits for them, and re-layouts: none -> 3.12 us  [the longest x2 2.16 us: body(): jnp.stack([key_sel.reshape(picked, D)] * lax.axis_size('seq'))]
    unnamed x30 -> x26, local copies, waits for them, and re-layouts: 6.73 us -> 6.71 us
  transfers between devices with their start and end apart: 2 -> 3, of which waited for: 2 -> 2; matrix products, arithmetic and copies ran while one was open for 7% -> 31% of each run, Pallas kernels for 0% -> 0%
where the time goes in v1:
time: 268 us; the launch traced here: 267 us
  local copies, waits for them, and re-layouts  69.1 us (26%)
  waiting for transfers between devices  62.6 us (23%)
  matrix products  52.1 us (19%)
  other arithmetic  38.7 us (14%)
  blocking collectives  16.1 us (6%)
  between operations  15 us (6%)
  loops' own time  6.92 us (3%)
  starting transfers between devices  6.69 us (2%)
    psum x1, waiting for transfers between devices, body(): lax.psum(shares.astype(jnp.bfloat16), 'dp').astype(jnp.float32)  39.2 us
    unnamed x3, waiting for transfers between devices  23.4 us
    dot_general x4, matrix products, one_group(): jnp.einsum('shqk,skhd->sqhd', weights.astype(jnp.bfloat16), value_part, p...  22.6 us
    broadcast_in_dim x4, local copies, waits for them, and re-layouts, combine(): jnp.where(dilation_match[None, :, :, None], dilated_row_sum[:, None], 0.0)  21.7 us
    another operation x3, local copies, waits for them, and re-layouts, select_rows(): tensor.reshape(segment_height // RATE, RATE, ATTENTION_HEADS, HEAD_SIZE)  21.5 us
    reduce_sum x4, other arithmetic, one_group(): totals = jnp.sum(weights, axis=-1)  16.4 us
    all_gather x1, blocking collectives, body(): lax.all_gather(value_sel.reshape(picked, D), 'seq', axis=0, tiled=True)  16.1 us
    dot_general x4, matrix products, one_group(): jnp.einsum('sqhd,skhd->shqk', query_part, key_part, preferred_element_typ...  13.4 us
  transfers between devices with their start and end apart: 3, of which 2 were waited for; matrix products, arithmetic and copies ran while one was open for 31% of the time, Pallas kernels for 0%

profile of v1, /device:TPU:0, one launch (start us, length us, event | category | flops | bytes accessed | tf_op | source)
XLA Modules:
  0.0 267.2 jit_solution(2130367453017860000)
XLA Ops:
  7.2 1.4 iota_compare_fusion
  8.6 2.8 %convolution_convert_fusion.3 = bf16[1024,768]{0,1:T(8,128)(2,1)S(1)} fusion(bf16[768,768]{1,0:T(8,128)(2,1)} %param.13, bf16[1,1024,768]{2,1,0:T(8,128)(2,1)S(1)} %copy-done), kind=kOutput, calls=%fused_computation.46 | convolution fusion | flops 1208745984 | bytes 4325376 | tf_op jit(solution)/shard_map/dot_general | solution.py:16
  11.5 2.6 convolution_convert_fusion.2
  14.1 2.6 convolution_convert_fusion.1
  16.7 2.7 %copy.49 = bf16[1024,768]{1,0:T(8,128)(2,1)} copy(bf16[1024,768]{0,1:T(8,128)(2,1)} %convolution_convert_fusion.1) | data formatting | bytes 3145728 | tf_op jit(solution)/shard_map/convert_element_type | solution.py:16
  19.4 1.6 copy.45
  21.0 1.6 copy.47
  22.6 7.2 %reshape_reshape.26 = bf16[64,16,16,48]{3,2,1,0:T(8,128)(2,1)} reshape(bf16[1024,768]{1,0:T(8,128)(2,1)} %copy.47) | data formatting | bytes 3145728 | tf_op jit(solution)/shard_map/reshape;reshape | solution.py:21
  29.8 7.2 %reshape_reshape.24 = bf16[64,16,16,48]{3,2,1,0:T(8,128)(2,1)} reshape(bf16[1024,768]{1,0:T(8,128)(2,1)} %copy.45) | data formatting | bytes 3145728 | tf_op jit(solution)/shard_map/reshape;reshape | solution.py:21
  37.0 7.2 %reshape_reshape.27 = bf16[64,16,16,48]{3,2,1,0:T(8,128)(2,1)} reshape(bf16[1024,768]{1,0:T(8,128)(2,1)} %copy.49) | data formatting | bytes 3145728 | tf_op jit(solution)/shard_map/reshape;reshape | solution.py:21
  44.1 9.0 %multiply_reduce_fusion.1 = (bf16[16,64,48]{2,0,1:T(8,128)(2,1)S(1)}, bf16[16,64,48]{2,0,1:T(8,128)(2,1)}, bf16[16,64,48]{2,0,1:T(8,128)(2,1)}) fusion(f32[16,16]{0,1:T(8,128)S(1)} %copy.80, bf16[64,16,16,48]{3,2,1,0:T(8,128)(2,1)} %reshape_reshape.26, bf16[64,16,16,48]{3,2,1,0:T(8,128)(2,1)} %reshape_reshape.27, bf16[64,16,16,48]{3,2,1,0:T(8,128)(2,1)} %reshape_reshape.24), kind=kLoop, calls=%fused_computation.25 | loop fusion | flops 6930432 | bytes 5014528
  53.1 1.2 stack_reshape.2
  54.3 0.9 stack.3
  55.3 6.4 %all-to-all-start = ((bf16[8,64,768]{2,1,0:T(8,128)(2,1)}), bf16[8,64,768]{2,1,0:T(8,128)(2,1)}, u32[]{:S(2)}, u32[]{:S(2)}) async-start(bf16[8,64,768]{2,1,0:T(8,128)(2,1)} %stack.3), calls=%async_computation | async-start | bytes 1572864 | tf_op jit(solution)/shard_map/all_to_all | solution.py:105
  61.7 66.5 %while.15 = (s32[]{:T(128)}, f32[4,1,4,1024]{3,2,1,0:T(4,128)S(1)}, f32[4,1,4,1024]{3,2,1,0:T(4,128)}, f32[4,1,1024,4,48]{2,4,3,1,0:T(8,128)}, s32[4]{0:T(128)S(...) while((s32[]{:T(128)}, f32[4,1,4,1024]{3,2,1,0:T(4,128)S(1)}, ...), condition=%wide.region_3.4_spmd.clone, body=%wide.region_0.3_spmd.clone.sunk | while | flops 851437568 | bytes 52434116 | solution.py:56
  61.7 0.6 dynamic_slice.41
  64.0 0.7 add_compare_fusion.4
  64.7 3.3 %fusion.70 = (f32[4,1024]{1,0:T(4,128)S(1)}, f32[4,1024,1024]{1,2,0:T(8,128)S(1)}) fusion(pred[1024]{0:T(1024)(128)(4,1)S(1)} %add_compare_fusion.4, bf16[1,1024,4,4,48]{1,4,3,2,0:T(8,128)(2,1)S(1)} %get-tuple-element.223, s32[]{:T(128)S(6)} %select_n.128, bf16[1,1024,4,4,48]{1,4,3,2,0:T(8,128)(2,1)S(1)} %get-tuple-element.222), kind=kOutput, calls=%fused_computation.3.clone.1 | convolution fusion | flops 415232000 | bytes 17582080 | tf_op jit(solution)/shard_map/while/body/eval_jaxpr/sqhd,skhd->shqk/dot_general | solution.py:41
  68.0 4.1 %fusion.71 = f32[4,1024]{1,0:T(4,128)S(1)} fusion(f32[4,1024,1024]{1,2,0:T(8,128)S(1)} %get-tuple-element.187, f32[4,1024]{1,0:T(4,128)S(1)} %get-tuple-element.188, pred[1024]{0:T(1024)(128)(4,1)S(1)} %add_compare_fusion.4), kind=kLoop, calls=%fused_computation.5.clone.1 | loop fusion | flops 16773120 | bytes 16811008 | tf_op jit(solution)/shard_map/while/body/eval_jaxpr/reduce_sum | solution.py:47
  72.1 5.7 %fusion.72 = f32[4,1,1024,4,48]{2,4,3,1,0:T(8,128)} fusion(f32[4,1,1024,4,48]{2,4,3,1,0:T(8,128)} %get-tuple-element.207, s32[]{:T(128)S(6)} %copy.89, f32[4,1024,1024]{1,2,0:T(8,128)S(1)} %get-tuple-element.187, f32[4,1024]{1,0:T(4,128)S(1)} %get-tuple-element.188, pred[1024]{0:T(1024)(128)(4,1)S(1)} %add_compare_fusion.4, ...), kind=kOutput, calls=%fused_computation.9.clone.1 | convolution fusion | flops 419430400 | bytes 17974280 | tf_op jit(solution)/shard_map/while/body/eval_jaxpr/shqk,skhd->sqhd/dot_general | solution.py:48
  77.8 0.6 bitcast_dynamic-update-slice_fusion.3
  78.4 0.6 dynamic_slice.41
  80.7 0.7 add_compare_fusion.4
  81.3 3.3 %fusion.70 = (f32[4,1024]{1,0:T(4,128)S(1)}, f32[4,1024,1024]{1,2,0:T(8,128)S(1)}) fusion(pred[1024]{0:T(1024)(128)(4,1)S(1)} %add_compare_fusion.4, bf16[1,1024,4,4,48]{1,4,3,2,0:T(8,128)(2,1)S(1)} %get-tuple-element.223, s32[]{:T(128)S(6)} %select_n.128, bf16[1,1024,4,4,48]{1,4,3,2,0:T(8,128)(2,1)S(1)} %get-tuple-element.222), kind=kOutput, calls=%fused_computation.3.clone.1 | convolution fusion | flops 415232000 | bytes 17582080 | tf_op jit(solution)/shard_map/while/body/eval_jaxpr/sqhd,skhd->shqk/dot_general | solution.py:41
  84.7 4.1 %fusion.71 = f32[4,1024]{1,0:T(4,128)S(1)} fusion(f32[4,1024,1024]{1,2,0:T(8,128)S(1)} %get-tuple-element.187, f32[4,1024]{1,0:T(4,128)S(1)} %get-tuple-element.188, pred[1024]{0:T(1024)(128)(4,1)S(1)} %add_compare_fusion.4), kind=kLoop, calls=%fused_computation.5.clone.1 | loop fusion | flops 16773120 | bytes 16811008 | tf_op jit(solution)/shard_map/while/body/eval_jaxpr/reduce_sum | solution.py:47
  88.8 5.6 %fusion.72 = f32[4,1,1024,4,48]{2,4,3,1,0:T(8,128)} fusion(f32[4,1,1024,4,48]{2,4,3,1,0:T(8,128)} %get-tuple-element.207, s32[]{:T(128)S(6)} %copy.89, f32[4,1024,1024]{1,2,0:T(8,128)S(1)} %get-tuple-element.187, f32[4,1024]{1,0:T(4,128)S(1)} %get-tuple-element.188, pred[1024]{0:T(1024)(128)(4,1)S(1)} %add_compare_fusion.4, ...), kind=kOutput, calls=%fused_computation.9.clone.1 | convolution fusion | flops 419430400 | bytes 17974280 | tf_op jit(solution)/shard_map/while/body/eval_jaxpr/shqk,skhd->sqhd/dot_general | solution.py:48
  94.4 0.6 bitcast_dynamic-update-slice_fusion.3
  95.0 0.6 dynamic_slice.41
  97.3 0.7 add_compare_fusion.4
  97.9 3.3 %fusion.70 = (f32[4,1024]{1,0:T(4,128)S(1)}, f32[4,1024,1024]{1,2,0:T(8,128)S(1)}) fusion(pred[1024]{0:T(1024)(128)(4,1)S(1)} %add_compare_fusion.4, bf16[1,1024,4,4,48]{1,4,3,2,0:T(8,128)(2,1)S(1)} %get-tuple-element.223, s32[]{:T(128)S(6)} %select_n.128, bf16[1,1024,4,4,48]{1,4,3,2,0:T(8,128)(2,1)S(1)} %get-tuple-element.222), kind=kOutput, calls=%fused_computation.3.clone.1 | convolution fusion | flops 415232000 | bytes 17582080 | tf_op jit(solution)/shard_map/while/body/eval_jaxpr/sqhd,skhd->shqk/dot_general | solution.py:41
  101.3 4.1 %fusion.71 = f32[4,1024]{1,0:T(4,128)S(1)} fusion(f32[4,1024,1024]{1,2,0:T(8,128)S(1)} %get-tuple-element.187, f32[4,1024]{1,0:T(4,128)S(1)} %get-tuple-element.188, pred[1024]{0:T(1024)(128)(4,1)S(1)} %add_compare_fusion.4), kind=kLoop, calls=%fused_computation.5.clone.1 | loop fusion | flops 16773120 | bytes 16811008 | tf_op jit(solution)/shard_map/while/body/eval_jaxpr/reduce_sum | solution.py:47
  105.4 5.6 %fusion.72 = f32[4,1,1024,4,48]{2,4,3,1,0:T(8,128)} fusion(f32[4,1,1024,4,48]{2,4,3,1,0:T(8,128)} %get-tuple-element.207, s32[]{:T(128)S(6)} %copy.89, f32[4,1024,1024]{1,2,0:T(8,128)S(1)} %get-tuple-element.187, f32[4,1024]{1,0:T(4,128)S(1)} %get-tuple-element.188, pred[1024]{0:T(1024)(128)(4,1)S(1)} %add_compare_fusion.4, ...), kind=kOutput, calls=%fused_computation.9.clone.1 | convolution fusion | flops 419430400 | bytes 17974280 | tf_op jit(solution)/shard_map/while/body/eval_jaxpr/shqk,skhd->sqhd/dot_general | solution.py:48
  111.0 0.6 bitcast_dynamic-update-slice_fusion.3
  111.6 0.6 dynamic_slice.41
  113.9 0.7 add_compare_fusion.4
  114.5 3.3 %fusion.70 = (f32[4,1024]{1,0:T(4,128)S(1)}, f32[4,1024,1024]{1,2,0:T(8,128)S(1)}) fusion(pred[1024]{0:T(1024)(128)(4,1)S(1)} %add_compare_fusion.4, bf16[1,1024,4,4,48]{1,4,3,2,0:T(8,128)(2,1)S(1)} %get-tuple-element.223, s32[]{:T(128)S(6)} %select_n.128, bf16[1,1024,4,4,48]{1,4,3,2,0:T(8,128)(2,1)S(1)} %get-tuple-element.222), kind=kOutput, calls=%fused_computation.3.clone.1 | convolution fusion | flops 415232000 | bytes 17582080 | tf_op jit(solution)/shard_map/while/body/eval_jaxpr/sqhd,skhd->shqk/dot_general | solution.py:41
  117.9 4.1 %fusion.71 = f32[4,1024]{1,0:T(4,128)S(1)} fusion(f32[4,1024,1024]{1,2,0:T(8,128)S(1)} %get-tuple-element.187, f32[4,1024]{1,0:T(4,128)S(1)} %get-tuple-element.188, pred[1024]{0:T(1024)(128)(4,1)S(1)} %add_compare_fusion.4), kind=kLoop, calls=%fused_computation.5.clone.1 | loop fusion | flops 16773120 | bytes 16811008 | tf_op jit(solution)/shard_map/while/body/eval_jaxpr/reduce_sum | solution.py:47
  122.0 5.6 %fusion.72 = f32[4,1,1024,4,48]{2,4,3,1,0:T(8,128)} fusion(f32[4,1,1024,4,48]{2,4,3,1,0:T(8,128)} %get-tuple-element.207, s32[]{:T(128)S(6)} %copy.89, f32[4,1024,1024]{1,2,0:T(8,128)S(1)} %get-tuple-element.187, f32[4,1024]{1,0:T(4,128)S(1)} %get-tuple-element.188, pred[1024]{0:T(1024)(128)(4,1)S(1)} %add_compare_fusion.4, ...), kind=kOutput, calls=%fused_computation.9.clone.1 | convolution fusion | flops 419430400 | bytes 17974280 | tf_op jit(solution)/shard_map/while/body/eval_jaxpr/shqk,skhd->sqhd/dot_general | solution.py:48
  127.6 0.6 bitcast_dynamic-update-slice_fusion.3
  128.9 0.3 broadcast_in_dim.147
  129.3 0.3 copy.70
  129.6 1.2 reshape.260
  130.8 16.1 %all_gather.3 = bf16[512,768]{1,0:T(8,128)(2,1)S(1)} all-gather(bf16[64,768]{1,0:T(8,128)(2,1)S(1)} %reshape.260), channel_id=1, replica_groups=mesh['dp'=4,'seq'=8] {'seq'}, dimensions={0}, use_global_device_ids=true | all-gather | bytes 884736 | tf_op jit(solution)/shard_map/all_gather | solution.py:110
  147.3 0.6 add_compare_fusion.2
  147.9 2.0 copy.46
  150.0 1.0 reshape_reshape.25
  150.9 0.6 bitcast_reduce_fusion
  151.6 0.8 fusion.34
  152.3 0.7 convolution_bitcast_fusion.1
  153.0 0.3 copy.51
  154.2 3.9 %broadcast_in_dim.156 = f32[64,16,16,48]{3,2,1,0:T(8,128)} broadcast(f32[64,16,48]{2,1,0:T(8,128)S(1)} %copy.51), dimensions={0,2,3} | broadcast | bytes 3342336 | tf_op jit(solution)/shard_map/jit(_where)/broadcast_in_dim | solution.py:74
  158.1 6.6 %copy.53 = f32[1024,16,48]{0,2,1:T(8,128)} copy(f32[1024,16,48]{2,1,0:T(8,128)} %bitcast.163) | data formatting | bytes 6291456 | tf_op jit(solution)/shard_map/jit(_where)/broadcast_in_dim | solution.py:74
  164.7 4.0 %fusion.32 = bf16[1024,16,48]{0,2,1:T(8,128)(2,1)S(1)} fusion(f32[1024,16,48]{0,2,1:T(8,128)} %copy.53, f32[4,1,1024,4,48]{2,4,3,1,0:T(8,128)} %get-tuple-element.52, f32[1024,16]{0,1:T(8,128)S(1)} %get-tuple-element.111, f32[1024,16]{0,1:T(8,128)S(1)} %get-tuple-element.113, f32[1024,16]{0,1:T(8,128)S(1)} %get-tuple-element.112, ...), kind=kLoop, calls=%fused_computation.37 | loop fusion | flops 5505024 | bytes 8078336 | tf_op jit(solution)/shard_map/convert_element_type | solution.py:84
  168.8 2.9 %convolution_bitcast_fusion = f32[768,768]{0,1:T(8,128)} fusion(bf16[1024,768]{0,1:T(8,128)(2,1)S(1)} %bitcast.167, bf16[1,1024,768]{2,1,0:T(8,128)(2,1)S(1)} %copy-done.8), kind=kOutput, calls=%fused_computation.42 | convolution fusion | flops 1207959552 | bytes 5505024 | tf_op jit(solution)/shard_map/tc,td->cd/dot_general | solution.py:133
  171.7 3.0 %copy.78 = f32[768,768]{1,0:T(8,128)} copy(f32[768,768]{0,1:T(8,128)} %convolution_bitcast_fusion) | data formatting | bytes 4718592
  174.8 0.3 all-reduce.2.cloned.1.call-start
  175.1 7.7 %broadcast_in_dim.157 = f32[1024,768]{1,0:T(8,128)} reshape(f32[64,16,16,48]{3,2,1,0:T(8,128)} %broadcast_in_dim.156) | data formatting | bytes 6291456 | tf_op jit(solution)/shard_map/jit(_where)/broadcast_in_dim | solution.py:74
  182.8 3.6 %copy.52 = f32[1024,768]{0,1:T(8,128)} copy(f32[1024,768]{1,0:T(8,128)} %broadcast_in_dim.157) | data formatting | bytes 6291456 | tf_op jit(solution)/shard_map/jit(_where)/broadcast_in_dim | solution.py:74
  186.4 3.8 %fusion.31 = bf16[1024,768]{0,1:T(8,128)(2,1)S(1)} fusion(f32[1024,768]{0,1:T(8,128)} %copy.52, f32[4,1,1024,4,48]{2,4,3,1,0:T(8,128)} %get-tuple-element.52, f32[1024,16]{0,1:T(8,128)S(1)} %get-tuple-element.111, f32[1024,16]{0,1:T(8,128)S(1)} %get-tuple-element.113, f32[1024,16]{0,1:T(8,128)S(1)} %get-tuple-element.112, ...), kind=kLoop, calls=%fused_computation.36 | loop fusion | flops 5505024 | bytes 8078336 | tf_op jit(solution)/shard_map/convert_element_type | solution.py:84
  190.2 23.4 %reduce-scatter.4.cloned.1.call-done = f32[96,768]{1,0:T(8,128)} async-done(((f32[768,768]{1,0:T(8,128)}), f32[96,768]{1,0:T(8,128)}) %reduce-scatter.4.cloned.1.call-update) | async-done | bytes 294928
  213.6 1.8 copy.79
  215.4 4.0 %fusion.40 = bf16[1,1024,768]{2,1,0:T(8,128)(2,1)} fusion(bf16[1024,768]{0,1:T(8,128)(2,1)S(1)} %fusion.31, bf16[768,768]{1,0:T(8,128)(2,1)} %param.16), kind=kOutput, calls=%fused_computation.53 | convolution fusion | flops 1208745984 | bytes 4325376 | tf_op jit(solution)/shard_map/dot_general | solution.py:130
  219.4 39.2 %all-reduce.2.cloned.1.call-done = bf16[768,96]{1,0:T(8,128)(2,1)} async-done(((bf16[768,96]{1,0:T(8,128)(2,1)}), bf16[768,96]{1,0:T(8,128)(2,1)}) %all-reduce.2.cloned.1.call-update) | async-done | bytes 147472 | tf_op jit(solution)/shard_map/psum | solution.py:138
  258.6 1.8 copy.54
  (43 shorter events, 1.6 us)
Async XLA Ops:
  7.2 1.5 copy-start
  8.6 2.8 %copy-start.9 = (bf16[768,768]{1,0:T(8,128)(2,1)S(1)}, bf16[768,768]{1,0:T(8,128)(2,1)}, u32[]{:S(2)}) copy-start(bf16[768,768]{1,0:T(8,128)(2,1)} %param.14) | copy-start | bytes 3538948
  11.5 2.6 copy-start.10
  16.7 2.7 %copy-start.2 = (bf16[1024,768]{0,1:T(8,128)(2,1)S(1)}, bf16[1024,768]{0,1:T(8,128)(2,1)}, u32[]{:S(2)}) copy-start(bf16[1024,768]{0,1:T(8,128)(2,1)} %convolution_convert_fusion.2) | copy-start | bytes 4718596
  55.3 92.7 %all-to-all-start = ((bf16[8,64,768]{2,1,0:T(8,128)(2,1)}), bf16[8,64,768]{2,1,0:T(8,128)(2,1)}, u32[]{:S(2)}, u32[]{:S(2)}) async-start(bf16[8,64,768]{2,1,0:T(8,128)(2,1)} %stack.3), calls=%async_computation | async-start | bytes 1572864 | tf_op jit(solution)/shard_map/all_to_all | solution.py:105
  61.6 152.0 %reduce-scatter.4.cloned.1.call-start = ((), (), s32[]{:S(2)}) async-start(), calls=%async_computation.3 | async-start | bytes 2654208
  61.7 67.2 %copy-start.6 = (pred[16,16]{0,1:T(8,128)(4,1)S(1)}, pred[16,16]{0,1:T(8,128)(4,1)}, u32[]{:S(2)}) copy-start(pred[16,16]{0,1:T(8,128)(4,1)} %get-tuple-element.118) | copy-start | bytes 772
  128.2 19.0 %copy-start.3 = (f32[4,1,4,1024]{3,2,1,0:T(4,128)S(1)}, f32[4,1,4,1024]{3,2,1,0:T(4,128)}, u32[]{:S(2)}) copy-start(f32[4,1,4,1024]{3,2,1,0:T(4,128)} %get-tuple-element.53) | copy-start | bytes 196612
  128.2 19.6 %copy-start.7 = (s32[16]{0:T(128)S(1)}, s32[16]{0:T(128)}, u32[]{:S(2)}) copy-start(s32[16]{0:T(128)} %param.12) | copy-start | bytes 196
  158.1 6.6 %copy-start.4 = (pred[1024]{0:T(1024)(128)(4,1)S(1)}, pred[1024]{0:T(1024)(128)(4,1)}, u32[]{:S(2)}) copy-start(pred[1024]{0:T(1024)(128)(4,1)} %add_compare_fusion.2) | copy-start | bytes 3076
  164.7 4.0 %copy-start.8 = (bf16[1,1024,768]{2,1,0:T(8,128)(2,1)S(1)}, bf16[1,1024,768]{2,1,0:T(8,128)(2,1)}, u32[]{:S(2)}) copy-start(bf16[1,1024,768]{2,1,0:T(8,128)(2,1)} %param.17) | copy-start | bytes 4718596
  174.8 83.8 %all-reduce.2.cloned.1.call-start = ((), (), s32[]{:S(2)}) async-start(), calls=%async_computation.2 | async-start | bytes 393216 | tf_op jit(solution)/shard_map/psum | solution.py:138
  182.8 3.6 %copy-start.5 = (pred[1024]{0:T(1024)(128)(4,1)S(1)}, pred[1024]{0:T(1024)(128)(4,1)}, u32[]{:S(2)}) copy-start(pred[1024]{0:T(1024)(128)(4,1)} %add_compare_fusion.2) | copy-start | bytes 3076
  215.4 44.9 %copy-start.1 = (bf16[1,1024,768]{2,1,0:T(8,128)(2,1)S(1)}, bf16[1,1024,768]{2,1,0:T(8,128)(2,1)}, u32[]{:S(2)}) copy-start(bf16[1,1024,768]{2,1,0:T(8,128)(2,1)} %param.10) | copy-start | bytes 4718596
Sparse Core Ops, SparseCore 0:
  174.9 38.6 reduce-scatter.3
  217.1 41.4 all-reduce.1
